TPU v7x, 256 devices: a whole 4x4x8 slice. The times are simulated.
256 devices in a mesh: seg: 8 (over x, z_lo), bond: 32 (over z_hi, y, core).
Axes of the slice: x: 4, y: 4, z: 8 (z_hi: 4, z_lo: 2; z = z_hi * 2 + z_lo), core: 2. Of those that a mesh axis runs over, the one named last changes fastest.
Arguments:
- last_sites: bfloat16 [8, 1024, 2048], P('seg', 'bond'), may hold values from -6 to 6
- first_sites: bfloat16 [8, 1024, 2048], P('seg', 'bond'), may hold values from -0.1875 to 0.1875
- start_basis: float32 [2048, 256], replicated, may hold values from -6 to 6
- fields: float32 [8, 2], replicated, may hold values from -3 to 3
- ranks: int32 [8], replicated, may hold values from 128 to 256
Outputs:
- new_left: float32 [8, 2048, 256], P('seg', 'bond')
- new_right: float32 [8, 256, 2048], P('seg')
All inputs are finite; a program needn't handle non-finite values.
Results may differ from a plain program's by a relative error of at most 0.00035.
Values may be sent and summed in bfloat16 or wider, within the bound.
A program may use at most 64 MiB of HBM per device.

v0:
```python
import jax
import jax.numpy as jnp
from jax import lax
from jax.sharding import Mesh
from jax.sharding import PartitionSpec as P

ITERS = 4
BOND = ("bond_0", "bond_1", "bond_2")


time_step = 0.5
anisotropy = 0.6


def padded_to(lines, peers):
    spare = -len(lines) % peers
    return jnp.pad(lines, [(0, spare)] + [(0, 0)] * (lines.ndim - 1))


def sent_to_all(x, axis):
    peers = lax.axis_size(axis)
    return lax.all_to_all(jnp.broadcast_to(x[None], (peers, *x.shape)), axis, 0, 0, tiled=True)


def laid_out(pieces, dim):
    pieces = jnp.moveaxis(pieces, 0, dim)
    lengths = pieces.shape
    return pieces.reshape(*lengths[:dim], lengths[dim] * lengths[dim + 1], *lengths[dim + 2 :])


def gathered_by_axis(x, axes, dim):
    far, near = axes
    initial = sent_to_all(x, far)
    pieces = jnp.swapaxes(sent_to_all(initial, near), 0, 1)
    return laid_out(pieces.reshape(-1, *x.shape), dim)


def split_up(x, dim, peers):
    before, after = (x.shape[:dim], x.shape[dim + 1 :])
    return jnp.moveaxis(x.reshape(*before, peers, -1, *after), dim, 0)


def sent_and_summed(x, axis, dim):
    peers = lax.axis_size(axis)
    pieces = lax.all_to_all(split_up(x, dim, peers), axis, 0, 0, tiled=True)
    return jnp.sum(pieces, axis=0)


def sum_by_axis(x, axes, dim):
    far, near = axes
    pieces = split_up(x, dim, lax.axis_size(far))
    nearer = sent_and_summed(pieces, near, dim + 1)
    arrived = lax.all_to_all(nearer, far, split_axis=0, concat_axis=0, tiled=True)
    return arrived.sum(axis=0)


def sum_by_parts(x, axes):
    lines = x.reshape(-1, x.shape[-1])
    padded = padded_to(lines, lax.axis_size(axes[0]) * lax.axis_size(axes[1]))
    whole = gathered_by_axis(sum_by_axis(padded, axes, 0), axes, 0)
    return lax.slice_in_dim(whole, 0, len(lines)).reshape(x.shape)


def passed_along(x, axis, by):
    peers = lax.axis_size(axis)
    return lax.ppermute(x, axis, [(i, (i + by) % peers) for i in range(peers)])


def bond_gate(pair):
    left_field = pair[0]
    right_field = pair[1]
    half_diff = 0.5 * (left_field - right_field)
    width = jnp.sqrt(half_diff * half_diff + 0.25)
    factor = jnp.exp(time_step * anisotropy / 4.0)
    cosine = jnp.cosh(time_step * width)
    ratio = jnp.sinh(time_step * width) / width
    total = left_field + right_field
    zero = jnp.zeros((), jnp.float32)
    first = jnp.exp(-time_step * (anisotropy / 4.0 + total / 2.0))
    last = jnp.exp(-time_step * (anisotropy / 4.0 - total / 2.0))
    middle = factor * (cosine - half_diff * ratio)
    other = factor * (cosine + half_diff * ratio)
    cross = -factor * ratio * 0.5
    rows = [
        jnp.stack([first, zero, zero, zero]),
        jnp.stack([zero, middle, cross, zero]),
        jnp.stack([zero, cross, other, zero]),
        jnp.stack([zero, zero, zero, last]),
    ]
    return jnp.stack(rows).reshape(2, 2, 2, 2)


def apply_gate(theta, pair):
    gate = bond_gate(pair)
    rows = theta.shape[0] // 2
    width = theta.shape[1] // 2
    four = theta.reshape(rows, 2, 2, width)
    mixed = jnp.einsum("pqrs,arsc->apqc", gate, four, precision=lax.Precision.HIGHEST)
    return mixed.reshape(rows * 2, width * 2)


def truncate(left, right, start_basis, pair, rank):
    local_rows = left.shape[0]
    bond_width = right.shape[1] // 2
    left_three = left.reshape(local_rows, 2, bond_width)
    piece = lax.all_gather(right, BOND, axis=0, tiled=True)
    theta = jnp.dot(
        left_three.reshape(local_rows * 2, piece.shape[0]),
        piece,
        preferred_element_type=jnp.float32,
    )
    mixed = apply_gate(theta, pair)
    unused = (jnp.arange(start_basis.shape[1], dtype=jnp.int32) >= rank).astype(jnp.float32)
    basis = start_basis * (1.0 - unused)[None, :]
    for step in range(ITERS):
        image = jnp.dot(mixed, basis, precision=lax.Precision.HIGHEST)
        partial_cols = lax.dot_general(
            mixed, image, (((0,), (0,)), ((), ())), precision=lax.Precision.HIGHEST
        )
        cols = sum_by_parts(partial_cols, (("bond_0", "bond_1"), "bond_2"))
        gram = jnp.dot(cols.T, cols, precision=lax.Precision.HIGHEST) + jnp.diag(unused)
        chol = jnp.linalg.cholesky(gram)
        basis = lax.linalg.triangular_solve(
            chol, cols, left_side=False, lower=True, transpose_a=True
        )
    left_factor = jnp.dot(mixed, basis, precision=lax.Precision.HIGHEST)
    right_factor = jnp.sqrt(jnp.float32(mixed.shape[1])) * basis.T
    return (left_factor, right_factor)


def per_device(last_sites, first_sites, start_basis, fields, ranks):
    segment = lax.axis_index("seg")
    count = lax.axis_size("seg")
    previous = passed_along(last_sites, "seg", 1)
    owner = (segment + count - 1) % count
    left_factor, right_factor = truncate(
        previous[0], first_sites[0], start_basis, fields[owner], ranks[owner]
    )
    new_left = passed_along(left_factor[None], "seg", -1)
    new_right = right_factor[None]
    return (new_left, new_right)


def solution(mesh):
    finer = Mesh(
        mesh.devices.reshape(mesh.shape["seg"], 4, 4, 2), ("seg", "bond_0", "bond_1", "bond_2")
    )
    return jax.shard_map(
        per_device,
        mesh=finer,
        in_specs=(P("seg", BOND, None), P("seg", BOND, None), P(), P(), P()),
        out_specs=(P("seg", BOND, None), P("seg", None, None)),
        check_vma=False,
    )
```

profile of v0, /device:TPU:1, one launch (start us, length us, event | category | flops | bytes accessed | tf_op | source)
XLA Modules:
  0.0 724.9 jit_solution(5119972270818223441)
XLA Ops:
  16.1 59.0 %all-gather.3.cloned.1.call-done = bf16[1,1024,2048]{2,1,0:T(8,128)(2,1)} async-done(((bf16[1,32,2048]{2,1,0:T(8,128)(2,1)}), bf16[1,1024,2048]{2,1,0:T(8,128)(2,1)}) %all-gather.3.cloned.1.call-update) | async-done | bytes 4194320 | tf_op jit(solution)/shard_map/all_gather | solution.py:106
  75.1 6.4 copy.55
  81.5 3.6 convolution_bitcast_fusion.4
  87.8 2.8 fusion.47
  92.7 6.2 all_to_all.80
  100.8 34.3 %all_to_all.88 = f32[16,64,256]{2,1,0:T(8,128)} all-to-all(f32[16,64,256]{2,1,0:T(8,128)S(1)} %reduce_sum.72), channel_id=1, replica_groups=mesh['seg'=8,'bond_0'=4,'bond_1'=4,'bond_2'=2] {'bond_0','bond_1'}, dimensions={0} | all-to-all | bytes 2097152 | tf_op jit(solution)/shard_map/all_to_all | solution.py:53
  137.5 5.1 all-to-all-start.2
  143.2 23.0 %all-to-all-done.2 = f32[16,64,256]{2,1,0:T(8,128)S(1)} async-done(((f32[16,64,256]{2,1,0:T(8,128)}), f32[16,64,256]{2,1,0:T(8,128)S(1)}, u32[]{:S(2)}, u32[]{:S(2)}) %all-to-all-start.2) | async-done | bytes 1048608 | tf_op jit(solution)/shard_map/all_to_all | solution.py:22
  166.4 7.3 %all_to_all.81 = f32[2,16,64,256]{3,2,1,0:T(8,128)S(1)} all-to-all(f32[2,16,64,256]{3,2,1,0:T(8,128)S(1)} %broadcast_in_dim.90), channel_id=1, replica_groups=mesh['seg'=8,'bond_0'=4,'bond_1'=4,'bond_2'=2] {'bond_2'}, dimensions={0} | all-to-all | bytes 4194304 | tf_op jit(solution)/shard_map/all_to_all | solution.py:22
  175.0 3.5 fusion.44
  178.6 11.7 %cholesky.214 = f32[128,128]{1,0:T(8,128)S(1)} custom-call(f32[128,128]{1,0:T(8,128)S(1)} %cholesky.346), custom_call_target="Cholesky" | custom-call | tf_op jit(solution)/shard_map/jit(cholesky)/cholesky | solution.py:122
  190.4 9.8 %custom-call.17 = f32[1,128,128]{1,2,0:T(8,128)S(1)} custom-call(f32[1,128,128]{2,1,0:T(8,128)S(1)} %get-tuple-element.89), custom_call_target="InvertDiagBlocksLowerTriangular" | custom-call | tf_op jit(solution)/shard_map/jit(cholesky)/cholesky | solution.py:122
  200.7 12.1 %cholesky.231 = f32[128,128]{1,0:T(8,128)S(1)} custom-call(f32[128,128]{1,0:T(8,128)S(1)} %convolution_subtract_fusion.7), custom_call_target="Cholesky" | custom-call | tf_op jit(solution)/shard_map/jit(cholesky)/cholesky | solution.py:122
  215.4 3.8 while.8
  219.2 19.7 %custom-call.18 = f32[2,128,128]{1,2,0:T(8,128)S(1)} custom-call(f32[2,128,128]{2,1,0:T(8,128)S(1)} %get-tuple-element.30), custom_call_target="InvertDiagBlocksLowerTriangular" | custom-call | tf_op jit(solution)/shard_map/triangular_solve/custom-call.0 | solution.py:123
  248.7 6.3 all_to_all.82
  256.9 27.8 %all_to_all.89 = f32[16,64,256]{2,1,0:T(8,128)} all-to-all(f32[16,64,256]{2,1,0:T(8,128)S(1)} %reduce_sum.74), channel_id=1, replica_groups=mesh['seg'=8,'bond_0'=4,'bond_1'=4,'bond_2'=2] {'bond_0','bond_1'}, dimensions={0} | all-to-all | bytes 2097152 | tf_op jit(solution)/shard_map/all_to_all | solution.py:53
  287.1 7.4 %all-to-all-start.6 = ((f32[16,64,256]{2,1,0:T(8,128)}), f32[16,64,256]{2,1,0:T(8,128)S(1)}, u32[]{:S(2)}, u32[]{:S(2)}) async-start(f32[16,64,256]{2,1,0:T(8,128)} %broadcast_in_dim.93), calls=%async_computation.6 | async-start | bytes 2097152 | tf_op jit(solution)/shard_map/all_to_all | solution.py:22
  294.5 19.9 %all-to-all-done.6 = f32[16,64,256]{2,1,0:T(8,128)S(1)} async-done(((f32[16,64,256]{2,1,0:T(8,128)}), f32[16,64,256]{2,1,0:T(8,128)S(1)}, u32[]{:S(2)}, u32[]{:S(2)}) %all-to-all-start.6) | async-done | bytes 1048608 | tf_op jit(solution)/shard_map/all_to_all | solution.py:22
  314.6 10.1 %all_to_all.83 = f32[2,16,64,256]{3,2,1,0:T(8,128)S(1)} all-to-all(f32[2,16,64,256]{3,2,1,0:T(8,128)S(1)} %broadcast_in_dim.94), channel_id=1, replica_groups=mesh['seg'=8,'bond_0'=4,'bond_1'=4,'bond_2'=2] {'bond_2'}, dimensions={0} | all-to-all | bytes 4194304 | tf_op jit(solution)/shard_map/all_to_all | solution.py:22
  326.0 3.5 fusion.41
  329.6 11.7 %cholesky.248 = f32[128,128]{1,0:T(8,128)S(1)} custom-call(f32[128,128]{1,0:T(8,128)S(1)} %cholesky.349), custom_call_target="Cholesky" | custom-call | tf_op jit(solution)/shard_map/jit(cholesky)/cholesky | solution.py:122
  341.4 9.8 %custom-call.19 = f32[1,128,128]{1,2,0:T(8,128)S(1)} custom-call(f32[1,128,128]{2,1,0:T(8,128)S(1)} %get-tuple-element.85), custom_call_target="InvertDiagBlocksLowerTriangular" | custom-call | tf_op jit(solution)/shard_map/jit(cholesky)/cholesky | solution.py:122
  351.7 12.1 %cholesky.265 = f32[128,128]{1,0:T(8,128)S(1)} custom-call(f32[128,128]{1,0:T(8,128)S(1)} %convolution_subtract_fusion.6), custom_call_target="Cholesky" | custom-call | tf_op jit(solution)/shard_map/jit(cholesky)/cholesky | solution.py:122
  366.4 3.8 while.9
  370.2 19.7 %custom-call.20 = f32[2,128,128]{1,2,0:T(8,128)S(1)} custom-call(f32[2,128,128]{2,1,0:T(8,128)S(1)} %get-tuple-element.31), custom_call_target="InvertDiagBlocksLowerTriangular" | custom-call | tf_op jit(solution)/shard_map/triangular_solve/custom-call.0 | solution.py:123
  399.7 6.3 all_to_all.84
  407.9 32.0 %all_to_all.90 = f32[16,64,256]{2,1,0:T(8,128)} all-to-all(f32[16,64,256]{2,1,0:T(8,128)S(1)} %reduce_sum.76), channel_id=1, replica_groups=mesh['seg'=8,'bond_0'=4,'bond_1'=4,'bond_2'=2] {'bond_0','bond_1'}, dimensions={0} | all-to-all | bytes 2097152 | tf_op jit(solution)/shard_map/all_to_all | solution.py:53
  442.2 7.0 all-to-all-start.10
  449.3 18.3 %all-to-all-done.10 = f32[16,64,256]{2,1,0:T(8,128)S(1)} async-done(((f32[16,64,256]{2,1,0:T(8,128)}), f32[16,64,256]{2,1,0:T(8,128)S(1)}, u32[]{:S(2)}, u32[]{:S(2)}) %all-to-all-start.10) | async-done | bytes 1048608 | tf_op jit(solution)/shard_map/all_to_all | solution.py:22
  467.8 11.6 %all_to_all.85 = f32[2,16,64,256]{3,2,1,0:T(8,128)S(1)} all-to-all(f32[2,16,64,256]{3,2,1,0:T(8,128)S(1)} %broadcast_in_dim.96), channel_id=1, replica_groups=mesh['seg'=8,'bond_0'=4,'bond_1'=4,'bond_2'=2] {'bond_2'}, dimensions={0} | all-to-all | bytes 4194304 | tf_op jit(solution)/shard_map/all_to_all | solution.py:22
  480.7 3.4 fusion.38
  484.4 11.7 %cholesky.282 = f32[128,128]{1,0:T(8,128)S(1)} custom-call(f32[128,128]{1,0:T(8,128)S(1)} %cholesky.352), custom_call_target="Cholesky" | custom-call | tf_op jit(solution)/shard_map/jit(cholesky)/cholesky | solution.py:122
  496.1 9.8 %custom-call.21 = f32[1,128,128]{1,2,0:T(8,128)S(1)} custom-call(f32[1,128,128]{2,1,0:T(8,128)S(1)} %get-tuple-element.81), custom_call_target="InvertDiagBlocksLowerTriangular" | custom-call | tf_op jit(solution)/shard_map/jit(cholesky)/cholesky | solution.py:122
  506.4 12.1 %cholesky.299 = f32[128,128]{1,0:T(8,128)S(1)} custom-call(f32[128,128]{1,0:T(8,128)S(1)} %convolution_subtract_fusion.5), custom_call_target="Cholesky" | custom-call | tf_op jit(solution)/shard_map/jit(cholesky)/cholesky | solution.py:122
  521.1 3.8 while.10
  524.9 19.7 %custom-call.22 = f32[2,128,128]{1,2,0:T(8,128)S(1)} custom-call(f32[2,128,128]{2,1,0:T(8,128)S(1)} %get-tuple-element.32), custom_call_target="InvertDiagBlocksLowerTriangular" | custom-call | tf_op jit(solution)/shard_map/triangular_solve/custom-call.0 | solution.py:123
  554.4 6.3 all_to_all.86
  562.6 32.6 %all_to_all.91 = f32[16,64,256]{2,1,0:T(8,128)S(1)} all-to-all(f32[16,64,256]{2,1,0:T(8,128)S(1)} %reduce_sum.78), channel_id=1, replica_groups=mesh['seg'=8,'bond_0'=4,'bond_1'=4,'bond_2'=2] {'bond_0','bond_1'}, dimensions={0} | all-to-all | bytes 2097152 | tf_op jit(solution)/shard_map/all_to_all | solution.py:53
  595.4 24.5 %all_to_all.92 = f32[16,64,256]{2,1,0:T(8,128)S(1)} all-to-all(f32[16,64,256]{2,1,0:T(8,128)S(1)} %broadcast_in_dim.97), channel_id=1, replica_groups=mesh['seg'=8,'bond_0'=4,'bond_1'=4,'bond_2'=2] {'bond_0','bond_1'}, dimensions={0} | all-to-all | bytes 2097152 | tf_op jit(solution)/shard_map/all_to_all | solution.py:22
  620.1 13.9 %all_to_all.87 = f32[2,16,64,256]{3,2,1,0:T(8,128)S(1)} all-to-all(f32[2,16,64,256]{3,2,1,0:T(8,128)S(1)} %broadcast_in_dim.98), channel_id=1, replica_groups=mesh['seg'=8,'bond_0'=4,'bond_1'=4,'bond_2'=2] {'bond_2'}, dimensions={0} | all-to-all | bytes 4194304 | tf_op jit(solution)/shard_map/all_to_all | solution.py:22
  635.3 3.5 fusion.35
  639.0 11.7 %cholesky.316 = f32[128,128]{1,0:T(8,128)S(1)} custom-call(f32[128,128]{1,0:T(8,128)S(1)} %cholesky.355), custom_call_target="Cholesky" | custom-call | tf_op jit(solution)/shard_map/jit(cholesky)/cholesky | solution.py:122
  650.8 9.8 %custom-call.23 = f32[1,128,128]{1,2,0:T(8,128)S(1)} custom-call(f32[1,128,128]{2,1,0:T(8,128)S(1)} %get-tuple-element.77), custom_call_target="InvertDiagBlocksLowerTriangular" | custom-call | tf_op jit(solution)/shard_map/jit(cholesky)/cholesky | solution.py:122
  661.1 11.9 %cholesky.333 = f32[128,128]{1,0:T(8,128)S(1)} custom-call(f32[128,128]{1,0:T(8,128)S(1)} %convolution_subtract_fusion.4), custom_call_target="Cholesky" | custom-call | tf_op jit(solution)/shard_map/jit(cholesky)/cholesky | solution.py:122
  675.7 4.1 while.11
  679.7 19.7 %custom-call.24 = f32[2,128,128]{1,2,0:T(8,128)S(1)} custom-call(f32[2,128,128]{2,1,0:T(8,128)S(1)} %get-tuple-element.33), custom_call_target="InvertDiagBlocksLowerTriangular" | custom-call | tf_op jit(solution)/shard_map/triangular_solve/custom-call.0 | solution.py:123
  707.2 8.4 %collective-permute-start.1 = (f32[1,64,256]{2,1,0:T(8,128)S(1)}, f32[1,64,256]{2,1,0:T(8,128)S(1)}, u32[]{:S(2)}, u32[]{:S(2)}) collective-permute-start(f32[1,64,256]{2,1,0:T(8,128)S(1)} %fusion.50), channel_id=1, source_target_pairs={{0,224},{32,0},{64,32},{96,64},{128,96},{160,128},{192,160},{224,1... | collective-permute-start | bytes 196616 | tf_op jit(solution)/shard_map/ppermute | solution.py:66
  (151 shorter events, 95.1 us)
Async XLA Ops:
  7.2 3.3 copy-start
  7.2 67.9 %all-gather.3.cloned.1.call-start = ((), (), s32[]{:S(2)}) async-start(), calls=%async_computation.16 | async-start | bytes 4325376 | tf_op jit(solution)/shard_map/all_gather | solution.py:106
  7.9 8.1 %collective-permute-start = (bf16[1,32,2048]{2,1,0:T(8,128)(2,1)}, bf16[1,32,2048]{2,1,0:T(8,128)(2,1)S(1)}, u32[]{:S(2)}, u32[]{:S(2)}) collective-permute-start(bf16[1,32,2048]{2,1,0:T(8,128)(2,1)} %param.8), channel_id=1, source_target_pairs={{0,32},{32,64},{64,96},{96,128},{128,160},{160,192},{192,224},{224... | collective-permute-start | bytes 393224 | tf_op jit(solution)/shard_map/ppermute | solution.py:66
  137.5 28.7 %all-to-all-start.2 = ((f32[16,64,256]{2,1,0:T(8,128)}), f32[16,64,256]{2,1,0:T(8,128)S(1)}, u32[]{:S(2)}, u32[]{:S(2)}) async-start(f32[16,64,256]{2,1,0:T(8,128)} %broadcast_in_dim.89), calls=%async_computation.2 | async-start | bytes 2097152 | tf_op jit(solution)/shard_map/all_to_all | solution.py:22
  173.7 1.3 copy-start.3
  287.1 27.3 %all-to-all-start.6 = ((f32[16,64,256]{2,1,0:T(8,128)}), f32[16,64,256]{2,1,0:T(8,128)S(1)}, u32[]{:S(2)}, u32[]{:S(2)}) async-start(f32[16,64,256]{2,1,0:T(8,128)} %broadcast_in_dim.93), calls=%async_computation.6 | async-start | bytes 2097152 | tf_op jit(solution)/shard_map/all_to_all | solution.py:22
  324.6 1.3 copy-start.4
  442.2 25.3 %all-to-all-start.10 = ((f32[16,64,256]{2,1,0:T(8,128)}), f32[16,64,256]{2,1,0:T(8,128)S(1)}, u32[]{:S(2)}, u32[]{:S(2)}) async-start(f32[16,64,256]{2,1,0:T(8,128)} %broadcast_in_dim.95), calls=%async_computation.10 | async-start | bytes 2097152 | tf_op jit(solution)/shard_map/all_to_all | solution.py:22
  479.4 1.3 copy-start.5
  634.0 1.3 copy-start.2
  705.2 12.6 %copy-start.1 = (f32[8,2]{0,1:T(2,128)S(1)}, f32[8,2]{0,1:T(2,128)}, u32[]{:S(2)}) copy-start(f32[8,2]{0,1:T(2,128)} %param.11) | copy-start | bytes 196
  707.2 10.0 %collective-permute-start.1 = (f32[1,64,256]{2,1,0:T(8,128)S(1)}, f32[1,64,256]{2,1,0:T(8,128)S(1)}, u32[]{:S(2)}, u32[]{:S(2)}) collective-permute-start(f32[1,64,256]{2,1,0:T(8,128)S(1)} %fusion.50), channel_id=1, source_target_pairs={{0,224},{32,0},{64,32},{96,64},{128,96},{160,128},{192,160},{224,1... | collective-permute-start | bytes 196616 | tf_op jit(solution)/shard_map/ppermute | solution.py:66
Sparse Core Ops, SparseCore 0:
  10.5 64.5 all-gather.2
where the time goes:
time: 733 us; the launch traced here: 725 us
  other arithmetic  233 us (32%)
  blocking collectives  219 us (30%)
  waiting for transfers between devices  121 us (17%)
  matrix products  55.6 us (8%)
  local copies, waits for them, and re-layouts  42.7 us (6%)
  starting transfers between devices  30.6 us (4%)
  between operations  22.7 us (3%)
    another operation x28, other arithmetic, truncate(): chol = jnp.linalg.cholesky(gram)  140 us
    all_to_all x4, blocking collectives, sum_by_axis(): lax.all_to_all(nearer, far, split_axis=0, concat_axis=0, tiled=True)  127 us
    another operation x9, other arithmetic, truncate(): lax.linalg.triangular_solve(chol, cols, left_side=False, lower=True, tran...  78.8 us
    all_to_all x5, blocking collectives, sent_to_all(): lax.all_to_all(jnp.broadcast_to(x[None], (peers, *x.shape)), axis, 0, 0,...  67.3 us
    all_to_all x3, waiting for transfers between devices, sent_to_all(): lax.all_to_all(jnp.broadcast_to(x[None], (peers, *x.shape)), axis, 0, 0,...  61.1 us
    all_gather x1, waiting for transfers between devices, truncate(): piece = lax.all_gather(right, BOND, axis=0, tiled=True)  59 us
    all_to_all x4, blocking collectives, sent_and_summed(): pieces = lax.all_to_all(split_up(x, dim, peers), axis, 0, 0, tiled=True)  25.1 us
    all_to_all x3, starting transfers between devices, sent_to_all(): lax.all_to_all(jnp.broadcast_to(x[None], (peers, *x.shape)), axis, 0, 0,...  19.6 us
  transfers between devices with their start and end apart: 6, of which 4 were waited for; matrix products, arithmetic and copies ran while one was open for 1% of the time, Pallas kernels for 0%

commit v1 on v0

v1 whole, which is shorter than its diff:
```python
import functools

import jax
import jax.numpy as jnp
from jax import lax
from jax.experimental import pallas as pl
from jax.experimental.pallas import tpu as pltpu
from jax.sharding import PartitionSpec as P

ITERS = 4
KEEP = 256
CHI = 1024
WIDE = 2048
ROWS = 64
Z, Y, CORES = 4, 4, 2

time_step = 0.5
anisotropy = 0.6
F32 = jnp.float32
BF16 = jnp.bfloat16


def halves(x):
    high = x.astype(BF16)
    return high, (x - high.astype(F32)).astype(BF16)


def dot(a, b, dims):
    return lax.dot_general(a, b, (dims, ((), ())), preferred_element_type=F32)


def splat(x, row, lane):
    return jnp.broadcast_to(x[row : row + 1, lane : lane + 1], (8, 128))


def eliminate_panel(work, factor, start):
    own = start // 128
    tiles = list(range(own, 2)) + [2 + t for t in range(own + 1)]
    sub = lax.broadcasted_iota(jnp.int32, (8, 128), 0)
    groups = 4
    x = [
        {t: work[start + 8 * h : start + 8 * h + 8, 128 * t : 128 * t + 128] for t in tiles}
        for h in range(groups)
    ]
    done = []
    for g in range(groups):
        lane = start % 128 + 8 * g
        rows = [
            {t: jnp.broadcast_to(x[g][t][i : i + 1, :], (8, 128)) for t in tiles} for i in range(8)
        ]
        a = {
            (u, t): jnp.broadcast_to(rows[u][own][:, lane + t : lane + t + 1], (8, 128))
            for u in range(8)
            for t in range(u + 1)
        }
        later = range(g + 1, groups)
        col = {
            (h, t): jnp.broadcast_to(x[h][own][:, lane + t : lane + t + 1], (8, 128))
            for h in later
            for t in range(8)
        }
        inverse = []
        for t in range(8):
            inverse.append(1.0 / a[t, t])
            for u in range(t + 1, 8):
                ratio = a[u, t] * inverse[t]
                for v in range(t + 1, u + 1):
                    a[u, v] = a[u, v] - ratio * a[v, t]
                for k in tiles:
                    rows[u][k] = rows[u][k] - ratio * rows[t][k]
                for h in later:
                    col[h, u] = col[h, u] - ratio * col[h, t]
        for h in later:
            for t in range(8):
                ratio = col[h, t] * inverse[t]
                for k in tiles:
                    x[h][k] = x[h][k] - ratio * rows[t][k]
        out = {}
        for t in range(8):
            guess = lax.rsqrt(a[t, t])
            scale = guess * (1.5 - 0.5 * a[t, t] * guess * guess)
            for k in tiles:
                value = rows[t][k] * scale
                out[k] = value if t == 0 else jnp.where(sub == t, value, out[k])
        for k in tiles:
            factor[start + 8 * g : start + 8 * g + 8, 128 * k : 128 * k + 128] = out[k]
        done.append(out)
    end = start + 32
    if end == KEEP:
        return
    panel = jnp.concatenate([jnp.concatenate([d[t] for t in tiles], axis=1) for d in done], axis=0)
    high, low = halves(panel)
    right = jnp.concatenate([high, high, low], axis=0)
    left = jnp.concatenate([high, low, high], axis=0)
    for t in range(own, 2):
        at = tiles.index(t) * 128
        first = max(end - 128 * t, 0)
        if first == 128:
            continue
        update = dot(left[:, at : at + 128], right, ((0,), (0,)))
        for n, k in enumerate(tiles):
            here = work[128 * t + first : 128 * t + 128, 128 * k : 128 * k + 128]
            work[128 * t + first : 128 * t + 128, 128 * k : 128 * k + 128] = (
                here - update[first:, 128 * n : 128 * n + 128]
            )


def gate_entries(left_field, right_field):
    hl = jnp.full((8, 128), left_field, F32)
    hr = jnp.full((8, 128), right_field, F32)
    half_diff = 0.5 * (hl - hr)
    width = jnp.sqrt(half_diff * half_diff + 0.25)
    factor = jnp.exp(jnp.full((8, 128), time_step * anisotropy / 4.0, F32))
    grow = jnp.exp(time_step * width)
    shrink = jnp.exp(-time_step * width)
    cosine = 0.5 * (grow + shrink)
    ratio = 0.5 * (grow - shrink) / width
    total = hl + hr
    first = jnp.exp(-time_step * (anisotropy / 4.0 + total / 2.0))
    last = jnp.exp(-time_step * (anisotropy / 4.0 - total / 2.0))
    middle = factor * (cosine - half_diff * ratio)
    other = factor * (cosine + half_diff * ratio)
    cross = -factor * ratio * 0.5
    return first, middle, cross, other, last


def kernel(
    last_ref,
    first_ref,
    start_ref,
    fields_ref,
    ranks_ref,
    left_out,
    right_out,
    right_all,
    left_all,
    mixed,
    a_rows,
    a_split,
    own_split,
    cols,
    parts,
    work,
    factor,
    prod,
    own_prod,
    left_stage,
    left_land,
    own_sem,
    pass_sem,
    r_send,
    r_recv,
    l_send,
    l_recv,
    c_send,
    c_recv,
    out_sem,
):
    seg = lax.axis_index("seg")
    bond = lax.axis_index("bond")
    z = bond // (Y * CORES)
    y = (bond // CORES) % Y
    c = bond % CORES
    owner = (seg + 7) % 8
    after = (seg + 1) % 8
    up = (y + 1) % Y
    down = (y + Y - 1) % Y
    across = (y + 2) % Y
    z_up = (z + 1) % Z
    z_down = (z + Z - 1) % Z
    z_across = (z + 2) % Z

    def place(zz, yy, cc):
        return {"bond": (zz * Y + yy) * CORES + cc}

    at_up, at_down = place(z, up, c), place(z, down, c)
    at_z_up, at_z_down = place(z_up, y, c), place(z_down, y, c)
    partner = place(z, y, 1 - c)

    barrier = pltpu.get_barrier_semaphore()
    for device in (at_up, at_down, at_z_up, at_z_down, partner, {"seg": owner}, {"seg": after}):
        pl.semaphore_signal(
            barrier, inc=1, device_id=device, device_id_type=pl.DeviceIdType.MESH
        )
    pl.semaphore_wait(barrier, 7)

    def remote(src, dst, send, recv, device):
        return pltpu.make_async_remote_copy(
            src_ref=src,
            dst_ref=dst,
            send_sem=send,
            recv_sem=recv,
            device_id=device,
            device_id_type=pl.DeviceIdType.MESH,
        )

    class SiteGather:
        def __init__(self, ref, own, send, recv):
            def copy(i, piece, device, source=None):
                return remote(piece if source is None else source, piece, send.at[i], recv.at[i], device)

            mine = ref.at[z, y, c]
            self.z_near = [copy(0, mine, at_z_up, own), copy(1, mine, at_z_down, own)]
            self.z_far = [
                copy(2, ref.at[z_down, y, c, pl.ds(0, 16)], at_z_up),
                copy(3, ref.at[z_up, y, c, pl.ds(16, 16)], at_z_down),
            ]
            order = (z, z_down, z_up, z_across)
            self.near = [
                [
                    copy(4 + 2 * j, ref.at[zz, y, c], at_up, own if j == 0 else None),
                    copy(5 + 2 * j, ref.at[zz, y, c], at_down, own if j == 0 else None),
                ]
                for j, zz in enumerate(order)
            ]
            self.far = [
                copy(12 + j, ref.at[zz, down, c], at_up)
                if j < 2
                else copy(12 + j, ref.at[zz, up, c], at_down)
                for j, zz in enumerate(order)
            ]
            self.core = [
                copy(16 + i, ref.at[:, yy, c], partner)
                for i, yy in enumerate((y, down, up, across))
            ]

        def z_first(self):
            for one in self.z_near:
                one.start()

        def y_first(self):
            for one in self.near[0]:
                one.start()

        def z_next(self):
            for one in self.z_near:
                one.wait_recv()
            for one in self.z_far:
                one.start()
            for j in (1, 2):
                for one in self.near[j]:
                    one.start()

        def z_last(self):
            for one in self.z_far:
                one.wait_recv()
            for one in self.near[3]:
                one.start()
            self.core[0].start()

        def forward(self, j):
            for one in self.near[j]:
                one.wait_recv()
            self.far[j].start()
            if j == 3:
                self.core[1].start()
                self.core[2].start()

        def across(self):
            for one in self.far:
                one.wait_recv()
            self.core[3].start()

        def drain(self):
            for one in (*self.z_near, *self.z_far, *self.far, *self.core):
                one.wait_send()
            for pair in self.near:
                for one in pair:
                    one.wait_send()

    passed = remote(last_ref.at[0], left_all.at[z, y, c], pass_sem.at[0], pass_sem.at[1], {"seg": after})
    passed.start()
    right_sites = SiteGather(right_all, first_ref.at[0], r_send, r_recv)
    left_sites = SiteGather(left_all, None, l_send, l_recv)
    right_sites.z_first()
    right_sites.y_first()
    own_copy = pltpu.make_async_copy(first_ref.at[0], right_all.at[z, y, c], own_sem)
    own_copy.start()
    passed.wait_recv()
    left_sites.z_first()
    own_copy.wait()
    right_sites.z_next()
    right_sites.z_last()
    left_sites.y_first()
    for j in range(4):
        right_sites.forward(j)
    left_sites.z_next()
    left_sites.z_last()
    right_sites.across()
    for one in right_sites.core:
        one.wait_recv()

    g_first, g_middle, g_cross, g_other, g_last = (
        g[0:1, 0:1] for g in gate_entries(fields_ref[owner, 0], fields_ref[owner, 1])
    )
    own_block = y * CORES + c
    window = pl.multiple_of(own_block * 256, 256)
    a_rows[...] = jnp.zeros_like(a_rows)

    def add_bundle(yy, cc):
        sites = left_all[:, yy, cc].reshape(128, WIDE)
        stacked = jnp.concatenate([sites[:, :CHI], sites[:, CHI:]], axis=0)

        def mix(i, carry):
            near = pl.ds(pl.multiple_of(i * 256, 256), 256)
            far = pl.ds(pl.multiple_of(CHI + i * 256, 256), 256)
            up_cols = right_all[:, :, :, :, near].reshape(CHI, 256)
            down_cols = right_all[:, :, :, :, far].reshape(CHI, 256)
            theta_up = dot(stacked, up_cols, ((1,), (0,)))
            theta_down = dot(stacked, down_cols, ((1,), (0,)))
            entries = [
                (0, near, g_first * theta_up[:128]),
                (0, far, g_middle * theta_down[:128] + g_cross * theta_up[128:]),
                (1, near, g_cross * theta_down[:128] + g_other * theta_up[128:]),
                (1, far, g_last * theta_down[128:]),
            ]
            for t, where, value in entries:
                high, low = halves(value)
                mixed[0, t, :, :, where] = high.reshape(Z, 32, 256)
                mixed[1, t, :, :, where] = low.reshape(Z, 32, 256)
            return carry

        lax.fori_loop(0, CHI // 256, mix, 0)
        high_rows = mixed[0, :, :, :, pl.ds(window, 256)].reshape(256, 256)
        low_rows = mixed[1, :, :, :, pl.ds(window, 256)].reshape(256, 256)
        both = jnp.concatenate([high_rows.T, low_rows.T], axis=0)

        def accumulate(i, carry):
            lanes = pl.ds(pl.multiple_of(i * 256, 256), 256)
            high = mixed[0, :, :, :, lanes].reshape(256, 256)
            low = mixed[1, :, :, :, lanes].reshape(256, 256)
            pair = dot(both, high, ((1,), (0,)))
            cross = dot(both[:256], low, ((1,), (0,)))
            a_rows[:, lanes] += pair[:256] + (pair[256:] + cross)
            return carry

        lax.fori_loop(0, WIDE // 256, accumulate, 0)

    add_bundle(y, c)
    for h in range(2):
        for t in range(2):
            own_split[h, 32 * t : 32 * t + 32, :] = mixed[h, t, z]
    for j in range(4):
        left_sites.forward(j)
    left_sites.core[0].wait_recv()
    add_bundle(y, 1 - c)
    add_bundle(down, c)
    left_sites.across()
    add_bundle(up, c)
    left_sites.core[1].wait_recv()
    add_bundle(down, 1 - c)
    left_sites.core[2].wait_recv()
    add_bundle(up, 1 - c)
    add_bundle(across, c)
    left_sites.core[3].wait_recv()
    add_bundle(across, 1 - c)
    passed.wait_send()
    right_sites.drain()
    left_sites.drain()

    rank = ranks_ref[owner]
    lane = lax.broadcasted_iota(jnp.int32, (1, KEEP), 1)
    used = (lane < rank).astype(F32)
    prod[...] = jnp.zeros_like(prod)

    def first_cols(i, carry):
        lines = pl.ds(pl.multiple_of(i * 256, 256), 256)
        top, rest = halves(a_rows[:, lines])
        a_split[0, :, lines] = top
        a_split[1, :, lines] = rest
        high, low = halves(start_ref[lines, :])
        prod[...] += dot(top, high, ((1,), (0,))) + (
            dot(rest, high, ((1,), (0,))) + dot(top, low, ((1,), (0,)))
        )
        return carry

    lax.fori_loop(0, WIDE // 256, first_cols, 0)
    high, low = halves(prod[...] * used)
    cols[0, y, c, 0] = high
    cols[0, y, c, 1] = low

    row_at = lax.broadcasted_iota(jnp.int32, (KEEP, KEEP), 0)
    lane_at = lax.broadcasted_iota(jnp.int32, (KEEP, KEEP), 1)
    diagonal = row_at == lane_at

    def iterate(step, carry):
        slot = step % 2

        def copy(i, piece, device):
            return remote(piece, piece, c_send.at[slot, i], c_recv.at[slot, i], device)

        def half(yy, h):
            return cols.at[slot, yy, c, h]

        near = [
            copy(0, half(y, 0), at_up),
            copy(1, half(y, 1), at_down),
            copy(2, half(y, 1), at_up),
            copy(3, half(y, 0), at_down),
        ]
        far = [copy(4, half(down, 0), at_up), copy(5, half(up, 1), at_down)]
        core = [
            copy(6, cols.at[slot, y, c], partner),
            copy(7, half(down, 0), partner),
            copy(8, half(up, 1), partner),
            copy(9, half(down, 1), partner),
            copy(10, half(up, 0), partner),
            copy(11, half(across, 0), partner),
            copy(12, half(across, 1), partner),
        ]

        def products(yy, cc):
            block = yy * CORES + cc
            high = cols[slot, yy, cc, 0]
            low = cols[slot, yy, cc, 1]
            parts[block] = dot(high, jnp.concatenate([high, low], axis=1), ((0,), (0,)))
            lanes = pl.ds(pl.multiple_of(block * 256, 256), 256)

            @pl.when(step < ITERS - 1)
            def _():
                rows = a_split[:, :, lanes].reshape(512, 256)
                pair = dot(rows, high, ((1,), (0,)))
                prod[...] += pair[:256] + (pair[256:] + dot(rows[:256], low, ((1,), (0,))))

            @pl.when(step == ITERS - 1)
            def _():
                rows = own_split[:, :, lanes].reshape(2 * ROWS, 256)
                pair = dot(rows, high, ((1,), (0,)))
                own_prod[...] += pair[:ROWS] + (
                    pair[ROWS:] + dot(rows[:ROWS], low, ((1,), (0,)))
                )

        for one in near:
            one.start()
        core[0].start()
        prod[...] = jnp.zeros_like(prod)
        own_prod[...] = jnp.zeros_like(own_prod)
        products(y, c)
        for i in range(2):
            near[i].wait_recv()
            far[i].start()
            core[1 + i].start()
        core[0].wait_recv()
        products(y, 1 - c)
        for i in range(2):
            near[2 + i].wait_recv()
            core[3 + i].start()
        products(down, c)
        products(up, c)
        for one in core[1:5]:
            one.wait_recv()
        products(down, 1 - c)
        products(up, 1 - c)
        for i in range(2):
            far[i].wait_recv()
            core[5 + i].start()
        products(across, c)
        for one in core[5:]:
            one.wait_recv()
        products(across, 1 - c)

        def total(i, carry):
            lines = pl.ds(pl.multiple_of(i * 32, 32), 32)
            value = parts[0, lines, :]
            for block in range(1, Y * CORES):
                value = value + parts[block, lines, :]
            work[lines, :] = value
            return carry

        lax.fori_loop(0, KEEP // 32, total, 0)
        unused = jnp.where(diagonal & (lane_at >= rank), 1.0, 0.0)
        cross = work[:, KEEP:]
        work[:, :KEEP] = work[:, :KEEP] + (cross + cross.T) + unused
        work[:, KEEP:] = jnp.where(diagonal, 1.0, 0.0)
        factor[...] = jnp.zeros_like(factor)
        for start in range(0, KEEP, 32):
            eliminate_panel(work, factor, start)
        for one in (*near, *far, *core):
            one.wait_send()

        @pl.when(step < ITERS - 1)
        def _():
            high, low = halves(factor[:, KEEP:])
            top, rest = halves(prod[...])
            value = dot(top, high, ((1,), (1,))) + (
                dot(top, low, ((1,), (1,))) + dot(rest, high, ((1,), (1,)))
            )
            top, rest = halves(value)
            cols[1 - slot, y, c, 0] = top
            cols[1 - slot, y, c, 1] = rest

        return carry

    lax.fori_loop(0, ITERS, iterate, 0)

    high, low = halves(factor[:, KEEP:])
    top, rest = halves(own_prod[...])
    own_prod[...] = dot(top, high, ((1,), (1,))) + (
        dot(top, low, ((1,), (1,))) + dot(rest, high, ((1,), (1,)))
    )
    for t in range(2):
        for n in range(2):
            left_stage.at[n][pl.ds(t, 32, stride=2), :] = own_prod[
                32 * t : 32 * t + 32, 128 * n : 128 * n + 128
            ]
    give = remote(left_stage, left_land, out_sem.at[0], out_sem.at[1], {"seg": owner})
    give.start()
    slot = (ITERS - 1) % 2
    inverse_high, inverse_low = halves(factor[:, KEEP:] * (float(WIDE) ** 0.5))

    def finish(i, carry):
        yy = i // CORES
        cc = i % CORES
        high = cols[slot, yy, cc, 0]
        low = cols[slot, yy, cc, 1]
        lanes = pl.ds(pl.multiple_of(i * 256, 256), 256)
        right_out[0, :, lanes] = dot(inverse_high, high, ((1,), (1,))) + (
            dot(inverse_low, high, ((1,), (1,))) + dot(inverse_high, low, ((1,), (1,)))
        )
        return carry

    lax.fori_loop(0, Y * CORES, finish, 0)
    give.wait()
    for n in range(2):
        left_out[0, :, 128 * n : 128 * n + 128] = left_land[n]


def per_device(last_sites, first_sites, start_basis, fields, ranks):
    vmem = pl.BlockSpec(memory_space=pltpu.VMEM)
    smem = pl.BlockSpec(memory_space=pltpu.SMEM)
    dma = pltpu.SemaphoreType.DMA
    return pl.pallas_call(
        kernel,
        out_shape=(
            jax.ShapeDtypeStruct((1, ROWS, KEEP), F32),
            jax.ShapeDtypeStruct((1, KEEP, WIDE), F32),
        ),
        in_specs=[vmem, vmem, vmem, smem, smem],
        out_specs=(vmem, vmem),
        scratch_shapes=[
            pltpu.VMEM((Z, Y, CORES, 32, WIDE), BF16),
            pltpu.VMEM((Z, Y, CORES, 32, WIDE), BF16),
            pltpu.VMEM((2, 2, Z, 32, WIDE), BF16),
            pltpu.VMEM((256, WIDE), F32),
            pltpu.VMEM((2, 256, WIDE), BF16),
            pltpu.VMEM((2, ROWS, WIDE), BF16),
            pltpu.VMEM((2, Y, CORES, 2, 256, KEEP), BF16),
            pltpu.VMEM((Y * CORES, KEEP, 2 * KEEP), F32),
            pltpu.VMEM((KEEP, 2 * KEEP), F32),
            pltpu.VMEM((KEEP, 2 * KEEP), F32),
            pltpu.VMEM((256, KEEP), F32),
            pltpu.VMEM((ROWS, KEEP), F32),
            pltpu.VMEM((2, ROWS, 128), F32),
            pltpu.VMEM((2, ROWS, 128), F32),
            dma,
            dma((2,)),
            dma((20,)),
            dma((20,)),
            dma((20,)),
            dma((20,)),
            dma((2, 13)),
            dma((2, 13)),
            dma((2,)),
        ],
        compiler_params=pltpu.CompilerParams(
            collective_id=0, has_side_effects=True, vmem_limit_bytes=60 * 1024 * 1024
        ),
    )(last_sites, first_sites, start_basis, fields, ranks)


def solution(mesh):
    return jax.shard_map(
        per_device,
        mesh=mesh,
        in_specs=(P("seg", "bond", None), P("seg", "bond", None), P(), P(), P()),
        out_specs=(P("seg", "bond", None), P("seg", None, None)),
        check_vma=False,
    )
```

time: 733 us -> 186 us (0.25); the launches traced: 725 us -> 186 us
  other arithmetic: 233 us -> 0 us
  blocking collectives: 219 us -> 0 us
  Pallas kernels: 0 us -> 179 us
  waiting for transfers between devices: 121 us -> 0 us
  matrix products: 55.6 us -> 0 us
  local copies, waits for them, and re-layouts: 42.7 us -> 5.95 us
  starting transfers between devices: 30.6 us -> 0 us
  between operations: 22.7 us -> 0.64 us
    all_to_all x13 -> x0, blocking collectives: 219 us -> none  [the longest x4 127 us: sum_by_axis(): lax.all_to_all(nearer, far, split_axis=0, concat_axis=0, tiled=True)]
    another operation x40 -> x0, other arithmetic: 219 us -> none  [the longest x28 140 us: truncate(): chol = jnp.linalg.cholesky(gram)]
    pallas_call x0 -> x1, Pallas kernels: none -> 179 us  [per_device(): pl.pallas_call(kernel, out_shape=(jax.ShapeDtypeStruct((1, ROWS, KEEP), F...]
    all_to_all x3 -> x0, waiting for transfers between devices: 61.1 us -> none  [sent_to_all(): lax.all_to_all(jnp.broadcast_to(x[None], (peers, *x.shape)), axis, 0, 0,...]
    all_gather x1 -> x0, waiting for transfers between devices: 59 us -> none  [truncate(): piece = lax.all_gather(right, BOND, axis=0, tiled=True)]
    dot_general x15 -> x0, matrix products: 37.7 us -> none  [the longest x4 13.8 us: truncate(): jnp.dot(cols.T, cols, precision=lax.Precision.HIGHEST) + jnp.diag(unused)]
    all_to_all x3 -> x0, starting transfers between devices: 19.6 us -> none  [sent_to_all(): lax.all_to_all(jnp.broadcast_to(x[None], (peers, *x.shape)), axis, 0, 0,...]
    another operation x20 -> x0, matrix products: 17.9 us -> none  [the longest x12 16 us: truncate(): lax.linalg.triangular_solve(chol, cols, left_side=False, lower=True, tran...]
  transfers between devices with their start and end apart: 6 -> 0, of which waited for: 4 -> 0; matrix products, arithmetic and copies ran while one was open for 1% -> 0% of each run, Pallas kernels for 0% -> 0%
where the time goes in v1:
time: 186 us
  Pallas kernels  179 us (96%)
  local copies, waits for them, and re-layouts  5.95 us (3%)
    pallas_call x1, Pallas kernels, per_device(): pl.pallas_call(kernel, out_shape=(jax.ShapeDtypeStruct((1, ROWS, KEEP), F...  179 us
    unnamed x3, local copies, waits for them, and re-layouts  5.95 us

profile of v1, /device:TPU:1, one launch (start us, length us, event | category | flops | bytes accessed | tf_op | source)
XLA Modules:
  0.0 185.9 jit_solution(7405900472962510350)
XLA Ops:
  0.6 1.3 copy.7.fields_ref
  2.0 179.3 %shard_map.68 = (f32[1,64,256]{2,1,0:T(8,128)}, f32[1,256,2048]{2,1,0:T(8,128)}) custom-call(bf16[1,32,2048]{2,1,0:T(8,128)(2,1)} %last_ref.1, bf16[1,32,2048]{2,1,0:T(8,128)(2,1)} %first_ref.1, f32[2048,256]{1,0:T(8,128)} %start_ref.1, f32[8,2]{1,0:T(8,128)} %copy.7.fields_ref, s32[8]{0:T(128)} %ranks_ref.1), custom_call_target="tpu_custom_call" | custom-call | tf_op jit(solution)/shard_map/pallas_call | solution.py:532
  181.3 1.5 copy.10
  182.8 3.1 %copy.11 = f32[1,256,2048]{2,1,0:T(8,128)} copy(f32[1,256,2048]{2,1,0:T(8,128)} %get-tuple-element.5) | data formatting | bytes 4194304

commit v2 on v1

v2 whole, which is shorter than its diff:
```python
import functools

import jax
import jax.numpy as jnp
from jax import lax
from jax.experimental import pallas as pl
from jax.experimental.pallas import tpu as pltpu
from jax.sharding import PartitionSpec as P

ITERS = 4
KEEP = 256
CHI = 1024
WIDE = 2048
ROWS = 64
Z, Y, CORES = 4, 4, 2

time_step = 0.5
anisotropy = 0.6
F32 = jnp.float32
BF16 = jnp.bfloat16


def halves(x):
    high = x.astype(BF16)
    return high, (x - high.astype(F32)).astype(BF16)


def dot(a, b, dims):
    return lax.dot_general(a, b, (dims, ((), ())), preferred_element_type=F32)


def splat(x, row, lane):
    return jnp.broadcast_to(x[row : row + 1, lane : lane + 1], (8, 128))


def eliminate_panel(work, factor, start):
    own = start // 128
    tiles = list(range(own, 2)) + [2 + t for t in range(own + 1)]
    sub = lax.broadcasted_iota(jnp.int32, (8, 128), 0)
    groups = 4
    x = [
        {t: work[start + 8 * h : start + 8 * h + 8, 128 * t : 128 * t + 128] for t in tiles}
        for h in range(groups)
    ]
    done = []
    for g in range(groups):
        lane = start % 128 + 8 * g
        rows = [
            {t: jnp.broadcast_to(x[g][t][i : i + 1, :], (8, 128)) for t in tiles} for i in range(8)
        ]
        a = {
            (u, t): jnp.broadcast_to(rows[u][own][:, lane + t : lane + t + 1], (8, 128))
            for u in range(8)
            for t in range(u + 1)
        }
        later = range(g + 1, groups)
        col = {
            (h, t): jnp.broadcast_to(x[h][own][:, lane + t : lane + t + 1], (8, 128))
            for h in later
            for t in range(8)
        }
        inverse = []
        for t in range(8):
            inverse.append(1.0 / a[t, t])
            for u in range(t + 1, 8):
                ratio = a[u, t] * inverse[t]
                for v in range(t + 1, u + 1):
                    a[u, v] = a[u, v] - ratio * a[v, t]
                for k in tiles:
                    rows[u][k] = rows[u][k] - ratio * rows[t][k]
                for h in later:
                    col[h, u] = col[h, u] - ratio * col[h, t]
        for h in later:
            for t in range(8):
                ratio = col[h, t] * inverse[t]
                for k in tiles:
                    x[h][k] = x[h][k] - ratio * rows[t][k]
        out = {}
        for t in range(8):
            guess = lax.rsqrt(a[t, t])
            scale = guess * (1.5 - 0.5 * a[t, t] * guess * guess)
            for k in tiles:
                value = rows[t][k] * scale
                out[k] = value if t == 0 else jnp.where(sub == t, value, out[k])
        for k in tiles:
            factor[start + 8 * g : start + 8 * g + 8, 128 * k : 128 * k + 128] = out[k]
        done.append(out)
    end = start + 32
    if end == KEEP:
        return
    panel = jnp.concatenate([jnp.concatenate([d[t] for t in tiles], axis=1) for d in done], axis=0)
    high, low = halves(panel)
    right = jnp.concatenate([high, high, low], axis=0)
    left = jnp.concatenate([high, low, high], axis=0)
    for t in range(own, 2):
        at = tiles.index(t) * 128
        first = max(end - 128 * t, 0)
        if first == 128:
            continue
        update = dot(left[:, at : at + 128], right, ((0,), (0,)))
        for n, k in enumerate(tiles):
            here = work[128 * t + first : 128 * t + 128, 128 * k : 128 * k + 128]
            work[128 * t + first : 128 * t + 128, 128 * k : 128 * k + 128] = (
                here - update[first:, 128 * n : 128 * n + 128]
            )


def gate_entries(left_field, right_field):
    hl = jnp.full((8, 128), left_field, F32)
    hr = jnp.full((8, 128), right_field, F32)
    half_diff = 0.5 * (hl - hr)
    width = jnp.sqrt(half_diff * half_diff + 0.25)
    factor = jnp.exp(jnp.full((8, 128), time_step * anisotropy / 4.0, F32))
    grow = jnp.exp(time_step * width)
    shrink = jnp.exp(-time_step * width)
    cosine = 0.5 * (grow + shrink)
    ratio = 0.5 * (grow - shrink) / width
    total = hl + hr
    first = jnp.exp(-time_step * (anisotropy / 4.0 + total / 2.0))
    last = jnp.exp(-time_step * (anisotropy / 4.0 - total / 2.0))
    middle = factor * (cosine - half_diff * ratio)
    other = factor * (cosine + half_diff * ratio)
    cross = -factor * ratio * 0.5
    return first, middle, cross, other, last


def kernel(
    last_ref,
    first_ref,
    start_ref,
    fields_ref,
    ranks_ref,
    left_out,
    right_out,
    right_all,
    left_all,
    stacked,
    mixed,
    start_split,
    image,
    scaled,
    sent,
    landed,
    cols,
    work,
    factor,
    left_stage,
    left_land,
    own_sem,
    pass_sem,
    r_send,
    r_recv,
    l_send,
    l_recv,
    s_send,
    s_recv,
    out_sem,
):
    seg = lax.axis_index("seg")
    bond = lax.axis_index("bond")
    z = bond // (Y * CORES)
    y = (bond // CORES) % Y
    c = bond % CORES
    owner = (seg + 7) % 8
    after = (seg + 1) % 8
    up = (y + 1) % Y
    down = (y + Y - 1) % Y
    across = (y + 2) % Y
    z_up = (z + 1) % Z
    z_down = (z + Z - 1) % Z
    z_across = (z + 2) % Z

    def place(zz, yy, cc):
        return {"bond": (zz * Y + yy) * CORES + cc}

    at_up, at_down = place(z, up, c), place(z, down, c)
    at_z_up, at_z_down, at_z_across = (place(zz, y, c) for zz in (z_up, z_down, z_across))
    partner = place(z, y, 1 - c)

    barrier = pltpu.get_barrier_semaphore()
    for device in (
        at_up,
        at_down,
        at_z_up,
        at_z_down,
        at_z_across,
        partner,
        {"seg": owner},
        {"seg": after},
    ):
        pl.semaphore_signal(
            barrier, inc=1, device_id=device, device_id_type=pl.DeviceIdType.MESH
        )
    pl.semaphore_wait(barrier, 8)

    def remote(src, dst, send, recv, device):
        return pltpu.make_async_remote_copy(
            src_ref=src,
            dst_ref=dst,
            send_sem=send,
            recv_sem=recv,
            device_id=device,
            device_id_type=pl.DeviceIdType.MESH,
        )

    class SiteGather:
        def __init__(self, ref, own, send, recv, cored):
            def copy(i, piece, device, source=None):
                return remote(piece if source is None else source, piece, send.at[i], recv.at[i], device)

            def at(zz, yy, *more):
                return ref.at[(zz, yy, c, *more) if cored else (zz, yy, *more)]

            mine = at(z, y)
            self.z = [
                copy(0, mine, at_z_down, own),
                copy(1, mine, at_z_up, own),
                copy(2, mine, at_z_across, own),
            ]
            order = (z, z_up, z_down, z_across)
            self.near = [
                [
                    copy(3 + 2 * j, at(zz, y), at_up, own if j == 0 else None),
                    copy(4 + 2 * j, at(zz, y), at_down, own if j == 0 else None),
                ]
                for j, zz in enumerate(order)
            ]
            self.far = [
                [
                    copy(11 + 2 * j, at(zz, down, pl.ds(0, 16)), at_up),
                    copy(12 + 2 * j, at(zz, up, pl.ds(16, 16)), at_down),
                ]
                for j, zz in enumerate(order)
            ]
            self.core = [
                copy(19 + i, ref.at[:, yy, c], partner)
                for i, yy in enumerate((y, down, up, across) if cored else ())
            ]

        def send_z(self):
            for one in self.z:
                one.start()

        def send_y(self, j):
            if j:
                self.z[j - 1].wait_recv()
            for one in self.near[j]:
                one.start()
            if j == 3:
                for one in self.core[:1]:
                    one.start()

        def forward(self, j):
            for i in range(2):
                self.near[j][i].wait_recv()
                self.far[j][i].start()
            if j == 3:
                for one in self.core[1:3]:
                    one.start()

        def across(self):
            for pair in self.far:
                for one in pair:
                    one.wait_recv()
            for one in self.core[3:]:
                one.start()

        def drain(self):
            for one in (*self.z, *self.core):
                one.wait_send()
            for pair in (*self.near, *self.far):
                for one in pair:
                    one.wait_send()

    passed = remote(last_ref.at[0], left_all.at[z, y], pass_sem.at[0], pass_sem.at[1], {"seg": after})
    passed.start()
    right_sites = SiteGather(right_all, first_ref.at[0], r_send, r_recv, True)
    left_sites = SiteGather(left_all, None, l_send, l_recv, False)
    right_sites.send_y(0)
    right_sites.send_z()
    own_copy = pltpu.make_async_copy(first_ref.at[0], right_all.at[z, y, c], own_sem)
    own_copy.start()
    passed.wait_recv()
    left_sites.send_y(0)
    left_sites.send_z()
    own_copy.wait()

    def split_start(i, carry):
        lines = pl.ds(pl.multiple_of(i * 256, 256), 256)
        high, low = halves(start_ref[lines, :])
        start_split[0, lines, :] = high
        start_split[1, lines, :] = low
        return carry

    lax.fori_loop(0, WIDE // 256, split_start, 0)
    right_sites.forward(0)
    right_sites.send_y(1)
    right_sites.send_y(2)
    left_sites.forward(0)
    right_sites.send_y(3)
    right_sites.forward(1)
    right_sites.forward(2)
    right_sites.forward(3)
    left_sites.send_y(1)
    left_sites.send_y(2)
    left_sites.send_y(3)
    right_sites.across()
    left_sites.forward(1)
    for one in right_sites.core:
        one.wait_recv()

    g_first, g_middle, g_cross, g_other, g_last = (
        g[0:1, 0:1] for g in gate_entries(fields_ref[owner, 0], fields_ref[owner, 1])
    )
    def add_bundle(yy):
        sites = left_all[:, yy].reshape(128, WIDE)
        stacked[:128] = sites[:, :CHI]
        stacked[128:] = sites[:, CHI:]

        def mix(i, carry):
            near = pl.ds(pl.multiple_of(i * 512, 512), 512)
            far = pl.ds(pl.multiple_of(CHI + i * 512, 512), 512)
            up_cols = right_all[:, :, :, :, near].reshape(CHI, 512)
            down_cols = right_all[:, :, :, :, far].reshape(CHI, 512)
            theta_up = dot(stacked[...], up_cols, ((1,), (0,)))
            theta_down = dot(stacked[...], down_cols, ((1,), (0,)))
            entries = [
                (0, near, g_first * theta_up[:128]),
                (0, far, g_middle * theta_down[:128] + g_cross * theta_up[128:]),
                (1, near, g_cross * theta_down[:128] + g_other * theta_up[128:]),
                (1, far, g_last * theta_down[128:]),
            ]
            for t, where, value in entries:
                high, low = halves(value)
                mixed[0, yy, t, :, where] = high
                mixed[1, yy, t, :, where] = low
            return carry

        lax.fori_loop(0, CHI // 512, mix, 0)
        rows = mixed[:, yy].reshape(512, WIDE)
        pair = dot(rows, start_split[0], ((1,), (0,)))
        cross = dot(rows[:256], start_split[1], ((1,), (0,)))
        image[yy] = pair[:256] + (pair[256:] + cross)

    add_bundle(y)
    left_sites.forward(2)
    left_sites.forward(3)
    add_bundle(down)
    left_sites.across()
    add_bundle(up)
    add_bundle(across)
    passed.wait_send()
    right_sites.drain()
    left_sites.drain()

    rank = ranks_ref[owner]
    row_at = lax.broadcasted_iota(jnp.int32, (KEEP, KEEP), 0)
    lane_at = lax.broadcasted_iota(jnp.int32, (KEEP, KEEP), 1)
    diagonal = row_at == lane_at
    factor[...] = jnp.zeros_like(factor)
    factor[:, KEEP:] = jnp.where(diagonal & (lane_at < rank), 1.0, 0.0)

    def iterate(step, carry):
        slot = step % 2
        swaps = [
            remote(sent.at[n], landed.at[slot, n], s_send.at[slot, n], s_recv.at[slot, n], partner)
            for n in range(4)
        ]
        top, rest = halves(factor[:, KEEP:])
        for n in range(4):
            high, low = halves(image[n])
            value = dot(top, high, ((1,), (1,))) + (
                dot(rest, high, ((1,), (1,))) + dot(top, low, ((1,), (1,)))
            )
            high, low = halves(value)
            scaled[:256, 256 * n : 256 * n + 256] = high
            scaled[256:, 256 * n : 256 * n + 256] = low
        for n in range(4):
            high = mixed[0, :, :, :, 512 * n : 512 * n + 512].reshape(CHI, 512)
            low = mixed[1, :, :, :, 512 * n : 512 * n + 512].reshape(CHI, 512)
            pair = dot(scaled[...], high, ((1,), (0,)))
            cross = dot(scaled[:256], low, ((1,), (0,)))
            sent[n] = pair[:256] + (pair[256:] + cross)
            swaps[n].start()
        work[...] = jnp.zeros_like(work)
        for n in range(4):
            swaps[n].wait_recv()
            high, low = halves(sent[n] + landed[slot, n])
            cols[0, :, 512 * n : 512 * n + 512] = high
            cols[1, :, 512 * n : 512 * n + 512] = low
            work[...] += dot(high, jnp.concatenate([high, low], axis=0), ((1,), (1,)))
        unused = jnp.where(diagonal & (lane_at >= rank), 1.0, 0.0)
        cross = work[:, KEEP:]
        work[:, :KEEP] = work[:, :KEEP] + (cross + cross.T) + unused
        work[:, KEEP:] = jnp.where(diagonal, 1.0, 0.0)
        factor[...] = jnp.zeros_like(factor)
        for p in range(8):
            eliminate_panel(work, factor, 32 * p)
            rows = mixed[:, p // 2, p % 2].reshape(256, WIDE)
            pair = dot(rows, cols[0], ((1,), (1,)))
            cross = dot(rows[:128], cols[1], ((1,), (1,)))
            image[p // 2, 128 * (p % 2) : 128 * (p % 2) + 128, :] = pair[:128] + (pair[128:] + cross)
        for one in swaps:
            one.wait_send()
        return carry

    lax.fori_loop(0, ITERS, iterate, 0)

    top, rest = halves(factor[:, KEEP:])
    for t in range(2):
        high, low = halves(image[y, pl.ds(pl.multiple_of(128 * t + 32 * z, 32), 32), :])
        value = dot(high, top, ((1,), (1,))) + (
            dot(high, rest, ((1,), (1,))) + dot(low, top, ((1,), (1,)))
        )
        for n in range(2):
            left_stage.at[n][pl.ds(t, 32, stride=2), :] = value[:, 128 * n : 128 * n + 128]
    give = remote(left_stage, left_land, out_sem.at[0], out_sem.at[1], {"seg": owner})
    give.start()
    top, rest = halves(factor[:, KEEP:] * (float(WIDE) ** 0.5))
    for n in range(4):
        lanes = slice(512 * n, 512 * n + 512)
        right_out[0, :, lanes] = dot(top, cols[0, :, lanes], ((1,), (0,))) + (
            dot(rest, cols[0, :, lanes], ((1,), (0,))) + dot(top, cols[1, :, lanes], ((1,), (0,)))
        )
    give.wait()
    for n in range(2):
        left_out[0, :, 128 * n : 128 * n + 128] = left_land[n]


def per_device(last_sites, first_sites, start_basis, fields, ranks):
    vmem = pl.BlockSpec(memory_space=pltpu.VMEM)
    smem = pl.BlockSpec(memory_space=pltpu.SMEM)
    dma = pltpu.SemaphoreType.DMA
    return pl.pallas_call(
        kernel,
        out_shape=(
            jax.ShapeDtypeStruct((1, ROWS, KEEP), F32),
            jax.ShapeDtypeStruct((1, KEEP, WIDE), F32),
        ),
        in_specs=[vmem, vmem, vmem, smem, smem],
        out_specs=(vmem, vmem),
        scratch_shapes=[
            pltpu.VMEM((Z, Y, CORES, 32, WIDE), BF16),
            pltpu.VMEM((Z, Y, 32, WIDE), BF16),
            pltpu.VMEM((256, CHI), BF16),
            pltpu.VMEM((2, Y, 2, 128, WIDE), BF16),
            pltpu.VMEM((2, WIDE, KEEP), BF16),
            pltpu.VMEM((Y, 256, KEEP), F32),
            pltpu.VMEM((512, CHI), BF16),
            pltpu.VMEM((4, KEEP, 512), F32),
            pltpu.VMEM((2, 4, KEEP, 512), F32),
            pltpu.VMEM((2, KEEP, WIDE), BF16),
            pltpu.VMEM((KEEP, 2 * KEEP), F32),
            pltpu.VMEM((KEEP, 2 * KEEP), F32),
            pltpu.VMEM((2, ROWS, 128), F32),
            pltpu.VMEM((2, ROWS, 128), F32),
            dma,
            dma((2,)),
            dma((23,)),
            dma((23,)),
            dma((19,)),
            dma((19,)),
            dma((2, 4)),
            dma((2, 4)),
            dma((2,)),
        ],
        compiler_params=pltpu.CompilerParams(
            collective_id=0, has_side_effects=True, vmem_limit_bytes=60 * 1024 * 1024
        ),
    )(last_sites, first_sites, start_basis, fields, ranks)


def solution(mesh):
    return jax.shard_map(
        per_device,
        mesh=mesh,
        in_specs=(P("seg", "bond", None), P("seg", "bond", None), P(), P(), P()),
        out_specs=(P("seg", "bond", None), P("seg", None, None)),
        check_vma=False,
    )
```

time: 186 us -> 132 us (0.71)
  Pallas kernels: 179 us -> 125 us
    pallas_call x1, Pallas kernels: 179 us -> 125 us  [per_device(): pl.pallas_call(kernel, out_shape=(jax.ShapeDtypeStruct((1, ROWS, KEEP), F...]
where the time goes in v2:
time: 132 us; the launch traced here: 131 us
  Pallas kernels  125 us (95%)
  local copies, waits for them, and re-layouts  5.95 us (5%)
    pallas_call x1, Pallas kernels, per_device(): pl.pallas_call(kernel, out_shape=(jax.ShapeDtypeStruct((1, ROWS, KEEP), F...  125 us
    unnamed x3, local copies, waits for them, and re-layouts  5.95 us

profile of v2, /device:TPU:1, one launch (start us, length us, event | category | flops | bytes accessed | tf_op | source)
XLA Modules:
  0.0 131.1 jit_solution(15801290759312019417)
XLA Ops:
  0.6 1.3 %copy.7.fields_ref = f32[8,2]{1,0:T(8,128)} copy(f32[8,2]{0,1:T(2,128)} %param.8) | data formatting | bytes 128 | tf_op args[3]
  2.0 124.5 %shard_map.68 = (f32[1,64,256]{2,1,0:T(8,128)}, f32[1,256,2048]{2,1,0:T(8,128)}) custom-call(bf16[1,32,2048]{2,1,0:T(8,128)(2,1)} %last_ref.1, bf16[1,32,2048]{2,1,0:T(8,128)(2,1)} %first_ref.1, f32[2048,256]{1,0:T(8,128)} %start_ref.1, f32[8,2]{1,0:T(8,128)} %copy.7.fields_ref, s32[8]{0:T(128)} %ranks_ref.1), custom_call_target="tpu_custom_call" | custom-call | tf_op jit(solution)/shard_map/pallas_call | solution.py:434
  126.5 1.5 %copy.10 = f32[1,64,256]{2,1,0:T(8,128)} copy(f32[1,64,256]{2,1,0:T(8,128)} %get-tuple-element.4) | data formatting | bytes 131072
  128.0 3.1 %copy.11 = f32[1,256,2048]{2,1,0:T(8,128)} copy(f32[1,256,2048]{2,1,0:T(8,128)} %get-tuple-element.5) | data formatting | bytes 4194304

commit v3 on v2

--- a/solution.py
+++ b/solution.py
@@ -155,6 +155,7 @@
     s_send,
     s_recv,
     out_sem,
+    write_sem,
 ):
     seg = lax.axis_index("seg")
     bond = lax.axis_index("bond")
@@ -310,7 +311,7 @@
         one.wait_recv()
 
     g_first, g_middle, g_cross, g_other, g_last = (
-        g[0:1, 0:1] for g in gate_entries(fields_ref[owner, 0], fields_ref[owner, 1])
+        g[0:1, 0:1] for g in gate_entries(fields_ref[0, owner], fields_ref[1, owner])
     )
     def add_bundle(yy):
         sites = left_all[:, yy].reshape(128, WIDE)
@@ -417,14 +418,22 @@
     give = remote(left_stage, left_land, out_sem.at[0], out_sem.at[1], {"seg": owner})
     give.start()
     top, rest = halves(factor[:, KEEP:] * (float(WIDE) ** 0.5))
+    writes = []
     for n in range(4):
         lanes = slice(512 * n, 512 * n + 512)
-        right_out[0, :, lanes] = dot(top, cols[0, :, lanes], ((1,), (0,))) + (
+        sent[n] = dot(top, cols[0, :, lanes], ((1,), (0,))) + (
             dot(rest, cols[0, :, lanes], ((1,), (0,))) + dot(top, cols[1, :, lanes], ((1,), (0,)))
         )
-    give.wait()
+        writes.append(pltpu.make_async_copy(sent.at[n], right_out.at[0, :, lanes], write_sem.at[n]))
+        writes[n].start()
+    give.wait_recv()
     for n in range(2):
-        left_out[0, :, 128 * n : 128 * n + 128] = left_land[n]
+        lanes = slice(128 * n, 128 * n + 128)
+        writes.append(pltpu.make_async_copy(left_land.at[n], left_out.at[0, :, lanes], write_sem.at[4 + n]))
+        writes[4 + n].start()
+    for one in writes:
+        one.wait()
+    give.wait_send()
 
 
 def per_device(last_sites, first_sites, start_basis, fields, ranks):
@@ -438,7 +447,7 @@
             jax.ShapeDtypeStruct((1, KEEP, WIDE), F32),
         ),
         in_specs=[vmem, vmem, vmem, smem, smem],
-        out_specs=(vmem, vmem),
+        out_specs=(pl.BlockSpec(memory_space=pl.ANY), pl.BlockSpec(memory_space=pl.ANY)),
         scratch_shapes=[
             pltpu.VMEM((Z, Y, CORES, 32, WIDE), BF16),
             pltpu.VMEM((Z, Y, 32, WIDE), BF16),
@@ -463,11 +472,12 @@
             dma((2, 4)),
             dma((2, 4)),
             dma((2,)),
+            dma((6,)),
         ],
         compiler_params=pltpu.CompilerParams(
             collective_id=0, has_side_effects=True, vmem_limit_bytes=60 * 1024 * 1024
         ),
-    )(last_sites, first_sites, start_basis, fields, ranks)
+    )(last_sites, first_sites, start_basis, fields.T, ranks)
 
 
 def solution(mesh):

time: 132 us -> 130 us (0.985)
  local copies, waits for them, and re-layouts: 5.95 us -> 4.61 us
    unnamed x3 -> x2, local copies, waits for them, and re-layouts: 5.95 us -> 4.61 us
where the time goes in v3:
time: 130 us; the launch traced here: 129 us
  Pallas kernels  124 us (95%)
  local copies, waits for them, and re-layouts  4.61 us (4%)
    pallas_call x1, Pallas kernels, per_device(): pl.pallas_call(kernel, out_shape=(jax.ShapeDtypeStruct((1, ROWS, KEEP), F...  124 us
    unnamed x2, local copies, waits for them, and re-layouts  4.61 us

profile of v3, /device:TPU:1, one launch (start us, length us, event | category | flops | bytes accessed | tf_op | source)
XLA Modules:
  0.0 129.1 jit_solution(13944966647656045230)
XLA Ops:
  0.6 123.9 %shard_map.68 = (f32[1,64,256]{2,1,0:T(8,128)}, f32[1,256,2048]{2,1,0:T(8,128)}) custom-call(bf16[1,32,2048]{2,1,0:T(8,128)(2,1)} %last_ref.1, bf16[1,32,2048]{2,1,0:T(8,128)(2,1)} %first_ref.1, f32[2048,256]{1,0:T(8,128)} %start_ref.1, f32[2,8]{1,0:T(2,128)} %bitcast.1, s32[8]{0:T(128)} %ranks_ref.1), custom_call_target="tpu_custom_call" | custom-call | tf_op jit(solution)/shard_map/pallas_call | solution.py:443
  124.5 1.5 %copy.9 = f32[1,64,256]{2,1,0:T(8,128)} copy(f32[1,64,256]{2,1,0:T(8,128)} %get-tuple-element.4) | data formatting | bytes 131072
  126.0 3.1 %copy.10 = f32[1,256,2048]{2,1,0:T(8,128)} copy(f32[1,256,2048]{2,1,0:T(8,128)} %get-tuple-element.5) | data formatting | bytes 4194304

commit v4 on v3

--- a/solution.py
+++ b/solution.py
@@ -396,11 +396,11 @@
         work[:, KEEP:] = jnp.where(diagonal, 1.0, 0.0)
         factor[...] = jnp.zeros_like(factor)
         for p in range(8):
-            eliminate_panel(work, factor, 32 * p)
             rows = mixed[:, p // 2, p % 2].reshape(256, WIDE)
             pair = dot(rows, cols[0], ((1,), (1,)))
             cross = dot(rows[:128], cols[1], ((1,), (1,)))
             image[p // 2, 128 * (p % 2) : 128 * (p % 2) + 128, :] = pair[:128] + (pair[128:] + cross)
+            eliminate_panel(work, factor, 32 * p)
         for one in swaps:
             one.wait_send()
         return carry

time: 130 us -> 130 us (level)
  no operation moved by 1% of the time
where the time goes in v4:
time: 130 us; the launch traced here: 129 us
  Pallas kernels  123 us (95%)
  local copies, waits for them, and re-layouts  4.61 us (4%)
    pallas_call x1, Pallas kernels, per_device(): pl.pallas_call(kernel, out_shape=(jax.ShapeDtypeStruct((1, ROWS, KEEP), F...  123 us
    unnamed x2, local copies, waits for them, and re-layouts  4.61 us

profile of v4, /device:TPU:1, one launch (start us, length us, event | category | flops | bytes accessed | tf_op | source)
XLA Modules:
  0.0 128.5 jit_solution(277455141622113171)
XLA Ops:
  0.6 123.3 %shard_map.68 = (f32[1,64,256]{2,1,0:T(8,128)}, f32[1,256,2048]{2,1,0:T(8,128)}) custom-call(bf16[1,32,2048]{2,1,0:T(8,128)(2,1)} %last_ref.1, bf16[1,32,2048]{2,1,0:T(8,128)(2,1)} %first_ref.1, f32[2048,256]{1,0:T(8,128)} %start_ref.1, f32[2,8]{1,0:T(2,128)} %bitcast.1, s32[8]{0:T(128)} %ranks_ref.1), custom_call_target="tpu_custom_call" | custom-call | tf_op jit(solution)/shard_map/pallas_call | solution.py:443
  123.9 1.5 %copy.9 = f32[1,64,256]{2,1,0:T(8,128)} copy(f32[1,64,256]{2,1,0:T(8,128)} %get-tuple-element.4) | data formatting | bytes 131072
  125.4 3.1 %copy.10 = f32[1,256,2048]{2,1,0:T(8,128)} copy(f32[1,256,2048]{2,1,0:T(8,128)} %get-tuple-element.5) | data formatting | bytes 4194304
